TPU v7x, 32 devices: a whole 2x2x4 slice. The times are simulated.
32 devices in a mesh: ctx: 8 (over y, x, core), fsdp: 4 (over z).
Axes of the slice: x: 2, y: 2, z: 4, core: 2. Of those that a mesh axis runs over, the one named last changes fastest.
Arguments:
- hidden_in: bfloat16 [4, 1024, 768], P('fsdp', 'ctx'), may hold values from -6 to 6
- out_grad: bfloat16 [4, 1024, 768], P('fsdp', 'ctx'), may hold values from -6 to 6
- block_ids: int32 [4, 1024], P('fsdp'), may hold values from 0 to 7, never falling along the last dimension, each value on 1 to 256 neighbouring positions
- clusters: int32 [4, 12, 1024], P('fsdp'), may hold values from 0 to 1023, as said below
- w_query: bfloat16 [768, 768], P('fsdp'), may hold values from -0.21875 to 0.21875
- w_key: bfloat16 [768, 768], P('fsdp'), may hold values from -0.21875 to 0.21875
- w_value: bfloat16 [768, 768], P('fsdp'), may hold values from -0.21875 to 0.21875
- w_out: bfloat16 [768, 768], P('fsdp'), may hold values from -1.25 to 1.25
- b_query: bfloat16 [768], P('fsdp'), may hold values from -3 to 3
- b_value: bfloat16 [768], P('fsdp'), may hold values from -3 to 3
- b_out: bfloat16 [768], P('fsdp'), may hold values from -3 to 3
- ln1_gain: bfloat16 [768], P('fsdp'), may hold values from 0.5 to 1.5
- ln1_bias: bfloat16 [768], P('fsdp'), may hold values from -3 to 3
- w_in: bfloat16 [768, 3072], P('fsdp'), may hold values from -0.21875 to 0.21875
- b_in: bfloat16 [3072], P('fsdp'), may hold values from -3 to 3
- w_down: bfloat16 [3072, 768], P('fsdp'), may hold values from -0.109375 to 0.109375
- b_down: bfloat16 [768], P('fsdp'), may hold values from -3 to 3
- ln2_gain: bfloat16 [768], P('fsdp'), may hold values from 0.5 to 1.5
- ln2_bias: bfloat16 [768], P('fsdp'), may hold values from -3 to 3
Outputs:
- layer_out: bfloat16 [4, 1024, 768], P('fsdp', 'ctx')
- input_grad: bfloat16 [4, 1024, 768], P('fsdp', 'ctx')
- grad_w_query: float32 [768, 768], P('fsdp')
- grad_w_key: float32 [768, 768], P('fsdp')
- grad_w_value: float32 [768, 768], P('fsdp')
- grad_w_out: float32 [768, 768], P('fsdp')
- grad_b_query: float32 [768], P('fsdp')
- grad_b_value: float32 [768], P('fsdp')
- grad_b_out: float32 [768], P('fsdp')
- grad_ln1_gain: float32 [768], P('fsdp')
- grad_ln1_bias: float32 [768], P('fsdp')
- grad_w_in: float32 [768, 3072], P('fsdp')
- grad_b_in: float32 [3072], P('fsdp')
- grad_w_down: float32 [3072, 768], P('fsdp')
- grad_b_down: float32 [768], P('fsdp')
- grad_ln2_gain: float32 [768], P('fsdp')
- grad_ln2_bias: float32 [768], P('fsdp')
Inputs may be any that keep to these rules, and one draw needn't show every extreme that they name: `clusters`: each head's row is an order of all 1024 stored rows of its sequence; every cluster (128 consecutive entries) holds exactly 16 stored rows of each aligned range of 128 stored rows. `block_ids`: never falls along the positions; each block holds 1 to 256 positions.
All inputs are finite; a program needn't handle non-finite values.
Results may differ from a plain program's by a relative error of at most 0.022.
Values may be sent and summed in bfloat16 or wider, within the bound.
No kernel may reach another device: no remote copies, remote signals or barrier semaphores. Data moves between devices by JAX's collectives and lax.ppermute only.
A program may use at most 192 MiB of HBM per device.

v0:
```python
import jax
import jax.numpy as jnp
from jax import lax
from jax.sharding import PartitionSpec as P

H = 12
DH = 64
CLUSTER = 128
EPSILON = 1e-12
FLOOR = -1e30


def layer_norm(values, gain, shift):
    centre = values - jnp.mean(values, axis=-1, keepdims=True)
    spread = jnp.mean(centre * centre, axis=-1, keepdims=True)
    return centre * lax.rsqrt(spread + EPSILON) * gain + shift


def exact_gelu(values):
    return jax.nn.gelu(values, approximate=False)


def positions(length, per_device, parts):
    stored = jnp.arange(length, dtype=jnp.int32)
    device = stored // per_device
    within = stored % per_device
    half = per_device // 2
    return jnp.where(
        within < half, device * half + within, (2 * parts - 1 - device) * half + within - half
    )


def contract(left, right):
    return lax.dot_general(
        left, right, (((0,), (0,)), ((), ())), preferred_element_type=jnp.float32
    )


def back_product(grad, weight):
    return lax.dot_general(
        grad, weight, (((1,), (1,)), ((), ())), preferred_element_type=jnp.float32
    )


def column_sum(values):
    return jnp.sum(values.astype(jnp.float32), axis=0)


def per_head_rows(rows, index):
    split = rows.reshape(rows.shape[0], H, DH)
    return jnp.take_along_axis(split, index.T[:, :, None], axis=0)


def cluster_tables(order, device, per_device, parts):
    heads, length = order.shape
    groups = length // CLUSTER
    members = CLUSTER // parts
    mine = (order // per_device == device).astype(jnp.int32)
    rank = jnp.cumsum(mine.reshape(heads, groups, CLUSTER), axis=-1).reshape(heads, length) - 1
    entry = jnp.arange(length, dtype=jnp.int32)[None, :]
    slot = jnp.where(mine == 1, entry // CLUSTER * members + rank, per_device)
    head_index = jnp.arange(heads, dtype=jnp.int32)[:, None]
    picked = (
        jnp.zeros((heads, per_device), jnp.int32)
        .at[head_index, slot]
        .set(order - device * per_device, mode="drop")
    )
    counter = jnp.broadcast_to(
        jnp.arange(per_device, dtype=jnp.int32)[None, :], (heads, per_device)
    )
    placed = jnp.zeros((heads, per_device), jnp.int32).at[head_index, picked].set(counter)
    inverse = (
        jnp.zeros((heads, length), jnp.int32)
        .at[head_index, order]
        .set(jnp.broadcast_to(jnp.arange(length, dtype=jnp.int32)[None, :], (heads, length)))
    )
    return (picked, placed, inverse)


def score_blocks(query, key_rows, query_blocks, key_blocks, scale):
    scores = (
        jnp.einsum("cqhd,ckhd->hcqk", query, key_rows, preferred_element_type=jnp.float32) * scale
    )
    allowed = key_blocks[:, :, None, :] <= query_blocks[:, :, :, None]
    return (scores, allowed)


def attend(query, key_rows, value_rows, query_blocks, key_blocks, scale):
    scores, allowed = score_blocks(query, key_rows, query_blocks, key_blocks, scale)
    masked = jnp.where(allowed, scores, FLOOR)
    top = jnp.max(masked, axis=-1, keepdims=True)
    weights = jnp.where(allowed, jnp.exp(masked - top), 0.0)
    total = jnp.sum(weights, axis=-1, keepdims=True)
    probs = (weights / total).astype(jnp.bfloat16)
    mixed = jnp.einsum("hcqk,ckhd->cqhd", probs, value_rows, preferred_element_type=jnp.float32)
    return (mixed.astype(jnp.bfloat16), top + jnp.log(total))


def attend_back(query, key_rows, value_rows, query_blocks, key_blocks, logsum, d_mixed, scale):
    scores, allowed = score_blocks(query, key_rows, query_blocks, key_blocks, scale)
    probs = jnp.where(allowed, jnp.exp(jnp.where(allowed, scores, FLOOR) - logsum), 0.0)
    rounded = probs.astype(jnp.bfloat16)
    d_probs = jnp.einsum("cqhd,ckhd->hcqk", d_mixed, value_rows, preferred_element_type=jnp.float32)
    centred = jnp.sum(probs * d_probs, axis=-1, keepdims=True)
    d_scores = (probs * (d_probs - centred)).astype(jnp.bfloat16)
    d_query = (
        jnp.einsum("hcqk,ckhd->cqhd", d_scores, key_rows, preferred_element_type=jnp.float32)
        * scale
    )
    d_key = (
        jnp.einsum("hcqk,cqhd->ckhd", d_scores, query, preferred_element_type=jnp.float32) * scale
    )
    d_value = jnp.einsum("hcqk,cqhd->ckhd", rounded, d_mixed, preferred_element_type=jnp.float32)
    return (d_query, d_key, d_value)


def body(
    hidden_in,
    out_grad,
    block_ids,
    clusters,
    w_query,
    w_key,
    w_value,
    w_out,
    b_query,
    b_value,
    b_out,
    ln1_gain,
    ln1_bias,
    w_in,
    b_in,
    w_down,
    b_down,
    ln2_gain,
    ln2_bias,
):
    parts = lax.axis_size("ctx")
    device = lax.axis_index("ctx")
    sequences, per_device, width = hidden_in.shape
    length = per_device * parts
    members = CLUSTER // parts
    groups = length // CLUSTER
    scale = DH ** (-0.5)
    (
        full_query,
        full_key,
        full_value,
        full_out,
        bias_query,
        bias_value,
        bias_out,
        gain_one,
        shift_one,
    ) = (
        lax.all_gather(w_query, "fsdp", axis=0, tiled=True),
        lax.all_gather(w_key, "fsdp", axis=0, tiled=True),
        lax.all_gather(w_value, "fsdp", axis=0, tiled=True),
        lax.all_gather(w_out, "fsdp", axis=0, tiled=True),
        lax.all_gather(b_query, "fsdp", axis=0, tiled=True),
        lax.all_gather(b_value, "fsdp", axis=0, tiled=True),
        lax.all_gather(b_out, "fsdp", axis=0, tiled=True),
        lax.all_gather(ln1_gain, "fsdp", axis=0, tiled=True),
        lax.all_gather(ln1_bias, "fsdp", axis=0, tiled=True),
    )
    full_in, full_down, bias_in, bias_down, gain_two, shift_two = (
        lax.all_gather(w_in, "fsdp", axis=0, tiled=True),
        lax.all_gather(w_down, "fsdp", axis=0, tiled=True),
        lax.all_gather(b_in, "fsdp", axis=0, tiled=True),
        lax.all_gather(b_down, "fsdp", axis=0, tiled=True),
        lax.all_gather(ln2_gain, "fsdp", axis=0, tiled=True),
        lax.all_gather(ln2_bias, "fsdp", axis=0, tiled=True),
    )
    hidden = hidden_in.reshape(sequences * per_device, width)
    query_rows = (
        jnp.dot(hidden, full_query, preferred_element_type=jnp.float32) + bias_query
    ).astype(jnp.bfloat16)
    key_rows = jnp.dot(hidden, full_key, preferred_element_type=jnp.float32).astype(jnp.bfloat16)
    value_rows = (
        jnp.dot(hidden, full_value, preferred_element_type=jnp.float32) + bias_value
    ).astype(jnp.bfloat16)
    place = positions(length, per_device, parts)
    index = 0
    order = clusters[index]
    stored_blocks = block_ids[index][place]
    picked, placed, inverse = cluster_tables(order, device, per_device, parts)
    q_local = per_head_rows(query_rows, picked).reshape(groups, members, H, DH)
    query_blocks = stored_blocks[device * per_device + picked].reshape(H, groups, members)
    key_all = lax.all_gather(key_rows, "ctx", axis=0, tiled=True)
    value_all = lax.all_gather(value_rows, "ctx", axis=0, tiled=True)
    key_cluster = per_head_rows(key_all, order).reshape(groups, CLUSTER, H, DH)
    value_cluster = per_head_rows(value_all, order).reshape(groups, CLUSTER, H, DH)
    key_blocks = stored_blocks[order].reshape(H, groups, CLUSTER)
    mixed, logsum = attend(q_local, key_cluster, value_cluster, query_blocks, key_blocks, scale)
    contexts = per_head_rows(mixed.reshape(per_device, width), placed).reshape(per_device, width)
    kept = [
        (
            q_local,
            key_cluster,
            value_cluster,
            query_blocks,
            key_blocks,
            logsum,
            picked,
            placed,
            inverse,
        )
    ]
    attended = jnp.dot(contexts, full_out, preferred_element_type=jnp.float32) + bias_out
    first_sum = hidden.astype(jnp.float32) + attended
    first, first_pull = jax.vjp(
        layer_norm, first_sum, gain_one.astype(jnp.float32), shift_one.astype(jnp.float32)
    )
    first_low = first.astype(jnp.bfloat16)
    inner = jnp.dot(first_low, full_in, preferred_element_type=jnp.float32) + bias_in
    active_full, gelu_pull = jax.vjp(exact_gelu, inner)
    active = active_full.astype(jnp.bfloat16)
    second_sum = first + jnp.dot(active, full_down, preferred_element_type=jnp.float32) + bias_down
    second, second_pull = jax.vjp(
        layer_norm, second_sum, gain_two.astype(jnp.float32), shift_two.astype(jnp.float32)
    )
    layer_out = second.astype(jnp.bfloat16).reshape(sequences, per_device, width)
    d_out = out_grad.reshape(sequences * per_device, width).astype(jnp.float32)
    d_second, g_gain_two, g_shift_two = second_pull(d_out)
    d_branch = d_second.astype(jnp.bfloat16)
    g_w_down = contract(active, d_branch)
    g_b_down = column_sum(d_branch)
    d_active = back_product(d_branch, full_down)
    d_inner = gelu_pull(d_active)[0].astype(jnp.bfloat16)
    g_w_in = contract(first_low, d_inner)
    g_b_in = column_sum(d_inner)
    d_first = d_second + back_product(d_inner, full_in)
    d_sum, g_gain_one, g_shift_one = first_pull(d_first)
    d_attended = d_sum.astype(jnp.bfloat16)
    g_w_out = contract(contexts, d_attended)
    g_b_out = column_sum(d_attended)
    d_context = back_product(d_attended, full_out).astype(jnp.bfloat16)
    index = 0
    q_kept, k_kept, v_kept, blocks_q, blocks_k, logsum, picked, placed, inverse = kept[index]
    d_cluster = per_head_rows(d_context, picked).reshape(groups, members, H, DH)
    d_query, d_key, d_value = attend_back(
        q_kept, k_kept, v_kept, blocks_q, blocks_k, logsum, d_cluster, scale
    )
    key_full = per_head_rows(d_key.reshape(length, width), inverse).reshape(length, width)
    value_full = per_head_rows(d_value.reshape(length, width), inverse).reshape(length, width)
    key_part = lax.psum_scatter(
        key_full.astype(jnp.bfloat16), "ctx", scatter_dimension=0, tiled=True
    )
    value_part = lax.psum_scatter(
        value_full.astype(jnp.bfloat16), "ctx", scatter_dimension=0, tiled=True
    )
    query_local = d_query.astype(jnp.bfloat16).reshape(per_device, width)
    query_grads = per_head_rows(query_local, placed).reshape(per_device, width)
    g_w_query = contract(hidden, query_grads)
    g_b_query = column_sum(query_grads)
    g_w_key = contract(hidden, key_part)
    g_w_value = contract(hidden, value_part)
    g_b_value = column_sum(value_part)
    input_total = (
        d_sum
        + back_product(query_grads, full_query)
        + back_product(key_part, full_key)
        + back_product(value_part, full_value)
    )
    input_grad = input_total.astype(jnp.bfloat16).reshape(sequences, per_device, width)
    shares = (
        lax.psum_scatter(
            g_w_query.astype(jnp.bfloat16), "fsdp", scatter_dimension=0, tiled=True
        ).astype(jnp.float32),
        lax.psum_scatter(
            g_w_key.astype(jnp.bfloat16), "fsdp", scatter_dimension=0, tiled=True
        ).astype(jnp.float32),
        lax.psum_scatter(
            g_w_value.astype(jnp.bfloat16), "fsdp", scatter_dimension=0, tiled=True
        ).astype(jnp.float32),
        lax.psum_scatter(
            g_w_out.astype(jnp.bfloat16), "fsdp", scatter_dimension=0, tiled=True
        ).astype(jnp.float32),
        lax.psum_scatter(
            g_b_query.astype(jnp.bfloat16), "fsdp", scatter_dimension=0, tiled=True
        ).astype(jnp.float32),
        lax.psum_scatter(
            g_b_value.astype(jnp.bfloat16), "fsdp", scatter_dimension=0, tiled=True
        ).astype(jnp.float32),
        lax.psum_scatter(
            g_b_out.astype(jnp.bfloat16), "fsdp", scatter_dimension=0, tiled=True
        ).astype(jnp.float32),
        lax.psum_scatter(
            g_gain_one.astype(jnp.bfloat16), "fsdp", scatter_dimension=0, tiled=True
        ).astype(jnp.float32),
        lax.psum_scatter(
            g_shift_one.astype(jnp.bfloat16), "fsdp", scatter_dimension=0, tiled=True
        ).astype(jnp.float32),
        lax.psum_scatter(
            g_w_in.astype(jnp.bfloat16), "fsdp", scatter_dimension=0, tiled=True
        ).astype(jnp.float32),
        lax.psum_scatter(
            g_b_in.astype(jnp.bfloat16), "fsdp", scatter_dimension=0, tiled=True
        ).astype(jnp.float32),
        lax.psum_scatter(
            g_w_down.astype(jnp.bfloat16), "fsdp", scatter_dimension=0, tiled=True
        ).astype(jnp.float32),
        lax.psum_scatter(
            g_b_down.astype(jnp.bfloat16), "fsdp", scatter_dimension=0, tiled=True
        ).astype(jnp.float32),
        lax.psum_scatter(
            g_gain_two.astype(jnp.bfloat16), "fsdp", scatter_dimension=0, tiled=True
        ).astype(jnp.float32),
        lax.psum_scatter(
            g_shift_two.astype(jnp.bfloat16), "fsdp", scatter_dimension=0, tiled=True
        ).astype(jnp.float32),
    )
    totals = (
        lax.psum(shares[0].astype(jnp.bfloat16), "ctx").astype(jnp.float32),
        lax.psum(shares[1].astype(jnp.bfloat16), "ctx").astype(jnp.float32),
        lax.psum(shares[2].astype(jnp.bfloat16), "ctx").astype(jnp.float32),
        lax.psum(shares[3].astype(jnp.bfloat16), "ctx").astype(jnp.float32),
        lax.psum(shares[4].astype(jnp.bfloat16), "ctx").astype(jnp.float32),
        lax.psum(shares[5].astype(jnp.bfloat16), "ctx").astype(jnp.float32),
        lax.psum(shares[6].astype(jnp.bfloat16), "ctx").astype(jnp.float32),
        lax.psum(shares[7].astype(jnp.bfloat16), "ctx").astype(jnp.float32),
        lax.psum(shares[8].astype(jnp.bfloat16), "ctx").astype(jnp.float32),
        lax.psum(shares[9].astype(jnp.bfloat16), "ctx").astype(jnp.float32),
        lax.psum(shares[10].astype(jnp.bfloat16), "ctx").astype(jnp.float32),
        lax.psum(shares[11].astype(jnp.bfloat16), "ctx").astype(jnp.float32),
        lax.psum(shares[12].astype(jnp.bfloat16), "ctx").astype(jnp.float32),
        lax.psum(shares[13].astype(jnp.bfloat16), "ctx").astype(jnp.float32),
        lax.psum(shares[14].astype(jnp.bfloat16), "ctx").astype(jnp.float32),
    )
    return (
        layer_out,
        input_grad,
        totals[0],
        totals[1],
        totals[2],
        totals[3],
        totals[4],
        totals[5],
        totals[6],
        totals[7],
        totals[8],
        totals[9],
        totals[10],
        totals[11],
        totals[12],
        totals[13],
        totals[14],
    )


def solution(mesh):
    in_specs = (
        P("fsdp", "ctx", None),
        P("fsdp", "ctx", None),
        P("fsdp", None),
        P("fsdp", None, None),
        P("fsdp", None),
        P("fsdp", None),
        P("fsdp", None),
        P("fsdp", None),
        P("fsdp"),
        P("fsdp"),
        P("fsdp"),
        P("fsdp"),
        P("fsdp"),
        P("fsdp", None),
        P("fsdp"),
        P("fsdp", None),
        P("fsdp"),
        P("fsdp"),
        P("fsdp"),
    )
    out_specs = (
        P("fsdp", "ctx", None),
        P("fsdp", "ctx", None),
        P("fsdp", None),
        P("fsdp", None),
        P("fsdp", None),
        P("fsdp", None),
        P("fsdp"),
        P("fsdp"),
        P("fsdp"),
        P("fsdp"),
        P("fsdp"),
        P("fsdp", None),
        P("fsdp"),
        P("fsdp", None),
        P("fsdp"),
        P("fsdp"),
        P("fsdp"),
    )
    return jax.shard_map(body, mesh=mesh, in_specs=in_specs, out_specs=out_specs, check_vma=False)
```

profile of v0, /device:TPU:0, one launch (start us, length us, event | category | flops | bytes accessed | tf_op | source)
XLA Modules:
  0.0 1361.8 jit_solution(14786672146078861802)
XLA Ops:
  17.3 21.1 %all-reduce.20 = (bf16[768]{0:T(1024)(128)(2,1)S(1)}, bf16[768]{0:T(1024)(128)(2,1)S(1)}, bf16[768]{0:T(1024)(128)(2,1)S(1)}, bf16[768]{0:T(1024)(128)(2,1)S(1)}...) all-reduce(bf16[768]{0:T(1024)(128)(2,1)S(1)} %dynamic-update-slice, ...), channel_id=1, replica_groups=mesh['ctx'=8,'fsdp'=4] {'fsdp'}, use_global_device_ids=true, to_apply=%add | all-reduce | flops 5376 | bytes 21504
  38.4 4.9 all-gather.10.cloned.1.call-done
  43.3 2.4 fusion.44
  45.8 28.7 %all-gather.16.cloned.1.call-done = bf16[768,768]{1,0:T(8,128)(2,1)} async-done(((bf16[192,768]{1,0:T(8,128)(2,1)}), bf16[768,768]{1,0:T(8,128)(2,1)}) %all-gather.16.cloned.1.call-update) | async-done | bytes 1179664 | tf_op jit(solution)/shard_map/all_gather | solution.py:157
  74.5 2.3 convolution_convert_fusion.7
  79.0 3.4 reduce_window_sum.11
  83.7 45.4 %scatter_custom_fusion = s32[1536]{0:T(1024)S(1)} fusion(s32[12288]{0:T(1024)S(1)} %reshape.537, s32[12288]{0:T(1024)S(1)} %reshape.539, s32[]{:T(128)} %constant.79.clone.1), kind=kCustom, calls=%fused_computation.202 | custom fusion | bytes 6148
  129.6 4.5 gather_fusion
  134.2 5.9 gather_fusion.2
  142.3 49.1 %gather_fusion.1 = s32[12288]{0:T(1024)S(1)} fusion(s32[1024]{0:T(1024)S(1)} %gather_fusion, s32[12288]{0:T(1024)S(1)} %broadcast_clamp_fusion), kind=kCustom, calls=%fused_computation.9 | custom fusion | bytes 147456 | tf_op jit(solution)/shard_map/gather | solution.py:193
  191.5 6.2 scatter_custom_fusion.1
  198.2 13.3 all-gather
  212.7 45.6 %scatter_custom_fusion.2 = s32[12288]{0:T(1024)S(1)} fusion(s32[12288]{0:T(1024)S(1)} %reshape.549, s32[12288]{0:T(1024)S(1)} %reshape.551, s32[]{:T(128)} %constant.79.clone.1), kind=kCustom, calls=%fused_computation.165 | custom fusion | bytes 49156
  261.6 8.5 gather_fusion.4
  271.5 2.6 copy.212
  274.1 3.1 copy.214
  277.1 119.4 %gather_fusion.3 = bf16[12288,64]{1,0:T(8,128)(2,1)} fusion(bf16[1024,12,64]{2,0,1:T(8,128)(2,1)S(1)} %copy.214, s32[12288]{0:T(1024)S(1)} %reshape.603), kind=kCustom, calls=%fused_computation.clone | custom fusion | bytes 3244032 | tf_op jit(solution)/shard_map/jit(take_along_axis)/gather | solution.py:51
  396.5 6.6 reshape.606
  403.1 2.6 copy.222
  405.7 3.1 copy.224
  408.7 119.3 %gather_fusion.5 = bf16[12288,64]{1,0:T(8,128)(2,1)} fusion(bf16[1024,12,64]{2,0,1:T(8,128)(2,1)S(1)} %copy.224, s32[12288]{0:T(1024)S(1)} %reshape.603), kind=kCustom, calls=%fused_computation.3.clone | custom fusion | bytes 3244032 | tf_op jit(solution)/shard_map/jit(take_along_axis)/gather | solution.py:51
  528.1 6.6 reshape.614
  534.7 10.9 broadcast_select_fusion
  545.7 1.9 fusion.103
  550.8 8.5 gather_fusion.6
  560.2 1.8 fusion.104
  562.3 8.6 multiply_convert_fusion
  571.0 3.6 fusion.105
  576.6 2.4 fusion.96
  580.0 2.4 multiply_reduce_fusion.1
  584.8 8.5 gather_fusion.7
  594.6 1.8 convolution_bitcast_fusion
  596.3 3.1 copy.268
  599.4 119.4 %gather_fusion.10 = bf16[12288,64]{1,0:T(8,128)(2,1)} fusion(bf16[1024,12,64]{2,0,1:T(8,128)(2,1)S(1)} %bitcast.190, s32[12288]{0:T(1024)S(1)} %reshape.627), kind=kCustom, calls=%fused_computation.7.clone | custom fusion | bytes 3244032 | tf_op jit(solution)/shard_map/jit(take_along_axis)/gather | solution.py:51
  718.8 6.6 reshape.634
  725.4 5.7 copy.255
  731.1 4.0 fusion.1
  735.1 8.4 fusion.32
  744.2 1.8 multiply_bitcast_fusion
  746.0 3.1 copy.266
  749.1 119.4 %gather_fusion.9 = bf16[12288,64]{1,0:T(8,128)(2,1)} fusion(bf16[1024,12,64]{2,0,1:T(8,128)(2,1)S(1)} %bitcast.189, s32[12288]{0:T(1024)S(1)} %reshape.627), kind=kCustom, calls=%fused_computation.2.clone | custom fusion | bytes 3244032 | tf_op jit(solution)/shard_map/jit(take_along_axis)/gather | solution.py:51
  868.5 6.6 reshape.630
  875.0 5.3 copy.249
  880.3 2.8 select_convert_fusion.1
  887.3 3.1 fusion.36
  890.5 8.5 gather_fusion.8
  901.9 20.9 %reduce-scatter.25.cloned.1.call-done = bf16[128,768]{1,0:T(8,128)(2,1)} async-done(((bf16[1024,768]{1,0:T(8,128)(2,1)}), bf16[128,768]{1,0:T(8,128)(2,1)}) %reduce-scatter.25.cloned.1.call-update) | async-done | bytes 196624
  925.7 39.2 %reduce-scatter.27.cloned.1.call-done = bf16[128,768]{1,0:T(8,128)(2,1)} async-done(((bf16[1024,768]{1,0:T(8,128)(2,1)}), bf16[128,768]{1,0:T(8,128)(2,1)}) %reduce-scatter.27.cloned.1.call-update) | async-done | bytes 196624
  969.7 3.7 convolution_convert_fusion.1
  974.5 3.6 convolution_convert_fusion
  978.2 18.2 %reduce-scatter.29.cloned.1.call-done = bf16[192,768]{1,0:T(8,128)(2,1)} async-done(((bf16[768,768]{1,0:T(8,128)(2,1)}), bf16[192,768]{1,0:T(8,128)(2,1)}) %reduce-scatter.29.cloned.1.call-update) | async-done | bytes 294928
  996.5 1.9 copy.274
  998.3 28.8 %reduce-scatter.31.cloned.1.call-done = bf16[192,768]{1,0:T(8,128)(2,1)} async-done(((bf16[768,768]{1,0:T(8,128)(2,1)}), bf16[192,768]{1,0:T(8,128)(2,1)}) %reduce-scatter.31.cloned.1.call-update) | async-done | bytes 294928
  1027.2 1.9 copy.276
  1029.0 28.9 %reduce-scatter.33.cloned.1.call-done = bf16[192,768]{1,0:T(8,128)(2,1)} async-done(((bf16[768,768]{1,0:T(8,128)(2,1)}), bf16[192,768]{1,0:T(8,128)(2,1)}) %reduce-scatter.33.cloned.1.call-update) | async-done | bytes 294928
  1058.0 1.9 copy.278
  1059.8 28.2 %reduce-scatter.19.cloned.1.call-done = bf16[192,768]{1,0:T(8,128)(2,1)} async-done(((bf16[768,768]{1,0:T(8,128)(2,1)}), bf16[192,768]{1,0:T(8,128)(2,1)}) %reduce-scatter.19.cloned.1.call-update) | async-done | bytes 294928 | tf_op jit(solution)/shard_map/reduce_scatter | solution.py:276
  1088.1 86.1 %reduce-scatter.21.cloned.1.call-done = bf16[192,3072]{1,0:T(8,128)(2,1)} async-done(((bf16[768,3072]{1,0:T(8,128)(2,1)}), bf16[192,3072]{1,0:T(8,128)(2,1)}) %reduce-scatter.21.cloned.1.call-update) | async-done | bytes 1179664 | tf_op jit(solution)/shard_map/reduce_scatter | solution.py:294
  1174.2 88.0 %reduce-scatter.23.cloned.1.call-done = bf16[768,768]{1,0:T(8,128)(2,1)} async-done(((bf16[3072,768]{1,0:T(8,128)(2,1)}), bf16[768,768]{1,0:T(8,128)(2,1)}) %reduce-scatter.23.cloned.1.call-update) | async-done | bytes 1179664 | tf_op jit(solution)/shard_map/reduce_scatter | solution.py:300
  1266.0 1.9 convolution_add_fusion.3
  1268.1 18.3 %all-reduce.19 = (bf16[768]{0:T(1024)(128)(2,1)S(1)}, bf16[768]{0:T(1024)(128)(2,1)S(1)}, bf16[768]{0:T(1024)(128)(2,1)S(1)}, bf16[768]{0:T(1024)(128)(2,1)S(1)}...) all-reduce(bf16[768]{0:T(1024)(128)(2,1)S(1)} %dynamic-update-slice, ...), channel_id=1, replica_groups=mesh['ctx'=8,'fsdp'=4] {'fsdp'}, use_global_device_ids=true, to_apply=%add.7 | all-reduce | flops 9984 | bytes 39936
  1287.1 12.0 all-reduce.17
  1307.9 38.7 %all-reduce.23.cloned.1.call-done = (bf16[192,768]{0,1:T(8,128)(2,1)}, bf16[192,768]{0,1:T(8,128)(2,1)}, bf16[192,768]{0,1:T(8,128)(2,1)}, bf16[192,768]{1,0:T(8...) async-done(((bf16[192,768]{0,1:T(8,128)(2,1)}, bf16[192,768]{0,1:T(8,128)(2,1)}, bf16[192,768]{0,1:T(8,128)(2,1)}, bf16[192,768]{1,0:T(8,128)(2,1)}, ...) | async-done | bytes 3538960 | tf_op jit(solution)/shard_map/psum | solution.py:314
  1346.6 3.0 convert_element_type.292
  (341 shorter events, 66.7 us)
Async XLA Ops:
  7.2 122.4 %copy-start = (s32[1,1024]{1,0:T(1,128)S(1)}, s32[1,1024]{1,0:T(1,128)}, u32[]{:S(2)}) copy-start(s32[1,1024]{1,0:T(1,128)} %param.27) | copy-start | bytes 12292
  7.2 67.3 %copy-start.8 = (bf16[1,128,768]{2,1,0:T(8,128)(2,1)S(1)}, bf16[1,128,768]{2,1,0:T(8,128)(2,1)}, u32[]{:S(2)}) copy-start(bf16[1,128,768]{2,1,0:T(8,128)(2,1)} %param.25) | copy-start | bytes 589828
  7.2 36.1 %all-gather.10.cloned.1.call-start = ((), (), s32[]{:S(2)}) async-start(), calls=%async_computation.8 | async-start | bytes 1474560 | tf_op jit(solution)/shard_map/all_gather | solution.py:158
  8.0 66.5 %all-gather.16.cloned.1.call-start = ((), (), s32[]{:S(2)}) async-start(), calls=%async_computation.11 | async-start | bytes 1474560 | tf_op jit(solution)/shard_map/all_gather | solution.py:157
  8.7 250.9 %all-gather.14.cloned.1.call-start = ((), (), s32[]{:S(2)}) async-start(), calls=%async_computation.10 | async-start | bytes 1474560 | tf_op jit(solution)/shard_map/all_gather | solution.py:156
  9.4 262.0 %all-gather.12.cloned.1.call-start = ((), (), s32[]{:S(2)}) async-start(), calls=%async_computation.9 | async-start | bytes 1769472 | tf_op jit(solution)/shard_map/all_gather | solution.py:190
  45.8 357.4 %all-gather.18.cloned.1.call-start = ((), (), s32[]{:S(2)}) async-start(), calls=%async_computation.12 | async-start | bytes 1769472 | tf_op jit(solution)/shard_map/all_gather | solution.py:189
  76.8 6.0 copy-start.63
  76.8 6.0 copy-start.68
  76.8 483.4 %all-gather.20.cloned.1.call-start = ((), (), s32[]{:S(2)}) async-start(), calls=%async_computation.13 | async-start | bytes 1474560 | tf_op jit(solution)/shard_map/all_gather | solution.py:159
  77.4 5.8 copy-start.64
  77.4 5.8 copy-start.67
  77.4 484.8 %all-gather.22.cloned.1.call-start = ((), (), s32[]{:S(2)}) async-start(), calls=%async_computation.14 | async-start | bytes 5898240 | tf_op jit(solution)/shard_map/all_gather | solution.py:167
  78.2 492.7 %all-gather.24.cloned.1.call-start = ((), (), s32[]{:S(2)}) async-start(), calls=%async_computation.15 | async-start | bytes 5898240 | tf_op jit(solution)/shard_map/all_gather | solution.py:168
  78.9 843.9 %reduce-scatter.25.cloned.1.call-start = ((), (), s32[]{:S(2)}) async-start(), calls=%async_computation.19 | async-start | bytes 1769472
  142.3 55.9 %copy-start.65 = (bf16[768]{0:T(1024)(128)(2,1)S(1)}, bf16[768]{0:T(1024)(128)(2,1)}, u32[]{:S(2)}) copy-start(bf16[768]{0:T(1024)(128)(2,1)} %param.39) | copy-start | bytes 4612
  270.6 3.5 copy-start.17
  528.1 6.6 copy-start.40
  534.7 11.0 copy-start.30
  534.7 11.0 copy-start.36
  545.7 5.1 copy-start.3
  562.0 20.4 %copy-start.4 = (f32[128,768]{1,0:T(8,128)}, f32[128,768]{1,0:T(8,128)S(1)}, u32[]{:S(2)}) copy-start(f32[128,768]{1,0:T(8,128)S(1)} %get-tuple-element.175) | copy-start | bytes 1179652
  562.2 20.2 %copy-start.49 = (f32[128]{0:T(128)}, f32[128]{0:T(128)S(1)}, u32[]{:S(2)}) copy-start(f32[128]{0:T(128)S(1)} %fusion.91) | copy-start | bytes 1540
  562.3 8.6 copy-start.48
  570.9 3.7 copy-start.11
  570.9 5.7 slice-start.2
  570.9 3.9 copy-start.27
  570.9 5.6 slice-start.3
  571.0 5.6 copy-start.70
  574.6 4.4 copy-start.58
  574.8 4.2 copy-start.61
  575.9 4.1 slice-start
  576.6 3.4 slice-start.1
  725.4 5.7 copy-start.31
  731.1 4.0 copy-start.10
  731.1 4.0 copy-start.46
  735.1 9.1 copy-start.18
  875.0 5.3 copy-start.47
  884.7 80.3 %reduce-scatter.27.cloned.1.call-start = ((), (), s32[]{:S(2)}) async-start(), calls=%async_computation.20 | async-start | bytes 1769472
  886.3 110.1 %reduce-scatter.29.cloned.1.call-start = ((), (), s32[]{:S(2)}) async-start(), calls=%async_computation.21 | async-start | bytes 1474560
  901.8 125.3 %reduce-scatter.31.cloned.1.call-start = ((), (), s32[]{:S(2)}) async-start(), calls=%async_computation.22 | async-start | bytes 1474560
  925.7 132.3 %reduce-scatter.33.cloned.1.call-start = ((), (), s32[]{:S(2)}) async-start(), calls=%async_computation.23 | async-start | bytes 1474560
  967.9 120.2 %reduce-scatter.19.cloned.1.call-start = ((), (), s32[]{:S(2)}) async-start(), calls=%async_computation.16 | async-start | bytes 1474560 | tf_op jit(solution)/shard_map/reduce_scatter | solution.py:276
  969.5 204.7 %reduce-scatter.21.cloned.1.call-start = ((), (), s32[]{:S(2)}) async-start(), calls=%async_computation.17 | async-start | bytes 5898240 | tf_op jit(solution)/shard_map/reduce_scatter | solution.py:294
  973.4 288.8 %reduce-scatter.23.cloned.1.call-start = ((), (), s32[]{:S(2)}) async-start(), calls=%async_computation.18 | async-start | bytes 5898240 | tf_op jit(solution)/shard_map/reduce_scatter | solution.py:300
  978.2 368.5 %all-reduce.23.cloned.1.call-start = ((), (), s32[]{:S(2)}) async-start(), calls=%async_computation.24 | async-start | bytes 7667712 | tf_op jit(solution)/shard_map/psum | solution.py:314
  1262.2 3.9 copy-start.14
  1262.2 3.9 copy-start.20
  1263.1 4.9 copy-start.29
  1263.1 4.9 copy-start.52
  1263.1 4.9 copy-start.53
  1263.1 41.2 %copy-start.13 = (bf16[768,768]{1,0:T(8,128)(2,1)S(1)}, bf16[768,768]{1,0:T(8,128)(2,1)}, u32[]{:S(2)}) copy-start(bf16[768,768]{1,0:T(8,128)(2,1)} %all-gather.16.cloned.1.call-done) | copy-start | bytes 3538948
  1263.1 41.2 %copy-start.37 = (bf16[128,768]{1,0:T(8,128)(2,1)S(1)}, bf16[128,768]{1,0:T(8,128)(2,1)}, u32[]{:S(2)}) copy-start(bf16[128,768]{1,0:T(8,128)(2,1)} %reduce-scatter.25.cloned.1.call-done) | copy-start | bytes 589828
  1263.8 4.3 copy-start.54
  1263.8 4.3 copy-start.55
  1263.8 4.3 copy-start.56
  1263.8 4.3 copy-start.57
  1263.8 4.3 copy-start.60
  1268.0 37.9 %copy-start.16 = (bf16[768,768]{1,0:T(8,128)(2,1)S(1)}, bf16[768,768]{1,0:T(8,128)(2,1)}, u32[]{:S(2)}) copy-start(bf16[768,768]{1,0:T(8,128)(2,1)} %all-gather.10.cloned.1.call-done) | copy-start | bytes 3538948
  1304.3 2.8 copy-start.7
  1304.3 2.8 copy-start.59
  1304.3 2.8 copy-start.62
  1346.6 3.0 copy-start.35
  1351.3 3.8 copy-start.1
  (28 other events, 46.2 us)
Sparse Core Ops, SparseCore 0:
  9.6 33.6 all-gather.9
  44.9 29.5 all-gather.15
  76.1 29.5 all-gather.13
  108.0 24.8 all-gather.11
  135.1 25.6 all-gather.17
  162.3 30.4 all-gather.19
  194.3 88.6 all-gather.21
  284.5 87.8 all-gather.23
  884.8 37.9 reduce-scatter.24
  926.5 38.4 reduce-scatter.26
  967.3 29.1 reduce-scatter.28
  999.2 27.9 reduce-scatter.30
  1030.0 27.8 reduce-scatter.32
  1060.1 27.8 reduce-scatter.18
  1090.2 83.9 reduce-scatter.20
  1176.4 85.7 reduce-scatter.22
  1267.3 79.2 all-reduce.22
where the time goes:
time: 1370 us; the launch traced here: 1360 us
  local copies, waits for them, and re-layouts  761 us (56%)
  waiting for transfers between devices  415 us (30%)
  blocking collectives  64.7 us (5%)
  matrix products  55.9 us (4%)
  other arithmetic  47.3 us (3%)
  between operations  17.5 us (1%)
    gather x26, local copies, waits for them, and re-layouts, per_head_rows(): return jnp.take_along_axis(split, index.T[:, :, None], axis=0)  551 us
    unnamed x22, waiting for transfers between devices  140 us
    unnamed x193, local copies, waits for them, and re-layouts  128 us
    reduce_scatter x1, waiting for transfers between devices, body(): lax.psum_scatter(g_w_down.astype(jnp.bfloat16), 'fsdp', scatter_dimension...  88 us
    reduce_scatter x1, waiting for transfers between devices, body(): lax.psum_scatter(g_w_in.astype(jnp.bfloat16), 'fsdp', scatter_dimension=0...  86.1 us
    gather x1, local copies, waits for them, and re-layouts, body(): key_blocks = stored_blocks[order].reshape(H, groups, CLUSTER)  49.1 us
    unnamed x2, blocking collectives  39.4 us
    psum x1, waiting for transfers between devices, body(): lax.psum(shares[0].astype(jnp.bfloat16), 'ctx').astype(jnp.float32)  38.7 us
  transfers between devices with their start and end apart: 17, of which 11 were waited for; matrix products, arithmetic and copies ran while one was open for 40% of the time, Pallas kernels for 0%

commit v1 on v0

--- a/solution.py
+++ b/solution.py
@@ -8,6 +8,18 @@
 CLUSTER = 128
 EPSILON = 1e-12
 FLOOR = -1e30
+
+
+def collect(x, axis, dim):
+    ways, here, step = (lax.axis_size(axis), lax.axis_index(axis), x.shape[dim])
+    line, have = (x, 1)
+    while have < ways:
+        line = jnp.concatenate(
+            [line, lax.ppermute(line, axis, [(d, (d - have) % ways) for d in range(ways)])],
+            axis=dim,
+        )
+        have = 2 * have
+    return jnp.roll(line, here * step, axis=dim)
 
 
 def layer_norm(values, gain, shift):
@@ -154,7 +166,7 @@
         shift_one,
     ) = (
         lax.all_gather(w_query, "fsdp", axis=0, tiled=True),
-        lax.all_gather(w_key, "fsdp", axis=0, tiled=True),
+        collect(w_key, "fsdp", 0),
         lax.all_gather(w_value, "fsdp", axis=0, tiled=True),
         lax.all_gather(w_out, "fsdp", axis=0, tiled=True),
         lax.all_gather(b_query, "fsdp", axis=0, tiled=True),

time: 1370 us -> 1390 us (1.015)
  waiting for transfers between devices: 415 us -> 432 us
    ppermute x0 -> x2, waiting for transfers between devices: none -> 51.5 us  [collect(): lax.ppermute(line, axis, [(d, (d - have) % ways) for d in range(ways)])]
    all_gather x1 -> x0, waiting for transfers between devices: 28.7 us -> none  [body(): lax.all_gather(w_key, 'fsdp', axis=0, tiled=True)]
    unnamed x193 -> x212, local copies, waits for them, and re-layouts: 128 us -> 124 us
    unnamed x22 -> x21, waiting for transfers between devices: 140 us -> 140 us
  transfers between devices with their start and end apart: 17 -> 18, of which waited for: 11 -> 11; matrix products, arithmetic and copies ran while one was open for 40% -> 39% of each run, Pallas kernels for 0% -> 0%
where the time goes in v1:
time: 1390 us; the launch traced here: 1380 us
  local copies, waits for them, and re-layouts  755 us (54%)
  waiting for transfers between devices  432 us (31%)
  blocking collectives  61.9 us (4%)
  matrix products  54.2 us (4%)
  other arithmetic  48.3 us (3%)
  between operations  17.6 us (1%)
    gather x26, local copies, waits for them, and re-layouts, per_head_rows(): return jnp.take_along_axis(split, index.T[:, :, None], axis=0)  551 us
    unnamed x21, waiting for transfers between devices  140 us
    unnamed x212, local copies, waits for them, and re-layouts  124 us
    reduce_scatter x1, waiting for transfers between devices, body(): lax.psum_scatter(g_w_in.astype(jnp.bfloat16), 'fsdp', scatter_dimension=0...  88 us
    reduce_scatter x1, waiting for transfers between devices, body(): lax.psum_scatter(g_w_down.astype(jnp.bfloat16), 'fsdp', scatter_dimension...  86.2 us
    ppermute x2, waiting for transfers between devices, collect(): lax.ppermute(line, axis, [(d, (d - have) % ways) for d in range(ways)])  51.5 us
    gather x1, local copies, waits for them, and re-layouts, body(): key_blocks = stored_blocks[order].reshape(H, groups, CLUSTER)  49.1 us
    psum x1, waiting for transfers between devices, body(): lax.psum(shares[0].astype(jnp.bfloat16), 'ctx').astype(jnp.float32)  38.1 us
  transfers between devices with their start and end apart: 18, of which 11 were waited for; matrix products, arithmetic and copies ran while one was open for 39% of the time, Pallas kernels for 0%

profile of v1, /device:TPU:0, one launch (start us, length us, event | category | flops | bytes accessed | tf_op | source)
XLA Modules:
  0.0 1376.7 jit_solution(6664510178466996806)
XLA Ops:
  8.7 5.1 collective-permute-start
  13.8 6.6 collective-permute-done
  22.9 45.0 %collective-permute-done.1 = bf16[384,768]{1,0:T(8,128)(2,1)S(1)} collective-permute-done((bf16[384,768]{1,0:T(8,128)(2,1)S(1)}, bf16[384,768]{1,0:T(8,128)(2,1)S(1)}, u32[]{:S(2)}, u32[]{:S(2)}) %collective-permute-start.1) | collective-permute-done | bytes 589856 | tf_op jit(solution)/shard_map/ppermute | solution.py:18
  73.8 17.0 %all-reduce.20 = (bf16[768]{0:T(1024)(128)(2,1)S(1)}, bf16[768]{0:T(1024)(128)(2,1)S(1)}, bf16[768]{0:T(1024)(128)(2,1)S(1)}, bf16[768]{0:T(1024)(128)(2,1)S(1)}...) all-reduce(bf16[768]{0:T(1024)(128)(2,1)S(1)} %dynamic-update-slice, ...), channel_id=1, replica_groups=mesh['ctx'=8,'fsdp'=4] {'fsdp'}, use_global_device_ids=true, to_apply=%add | all-reduce | flops 5376 | bytes 21504
  90.8 2.3 fusion.46
  95.1 3.4 reduce_window_sum.11
  99.9 45.4 %scatter_custom_fusion = s32[1536]{0:T(1024)S(1)} fusion(s32[12288]{0:T(1024)S(1)} %reshape.537, s32[12288]{0:T(1024)S(1)} %reshape.539, s32[]{:T(128)} %constant.101.clone.1), kind=kCustom, calls=%fused_computation.212 | custom fusion | bytes 6148
  147.3 4.5 gather_fusion
  151.8 5.9 gather_fusion.2
  158.4 49.1 %gather_fusion.1 = s32[12288]{0:T(1024)S(1)} fusion(s32[1024]{0:T(1024)S(1)} %gather_fusion, s32[12288]{0:T(1024)S(1)} %broadcast_clamp_fusion), kind=kCustom, calls=%fused_computation.9 | custom fusion | bytes 147456 | tf_op jit(solution)/shard_map/gather | solution.py:205
  207.6 6.2 scatter_custom_fusion.1
  214.3 14.1 %all-gather = bf16[4,1,768]{2,1,0:T(2,128)(2,1)S(1)} all-gather(bf16[1,1,768]{2,1,0:T(2,128)(2,1)S(1)} %reshape.584), channel_id=1, replica_groups=mesh['ctx'=8,'fsdp'=4] {'fsdp'}, dimensions={0}, use_global_device_ids=true | all-gather | bytes 7680 | tf_op jit(solution)/shard_map/all_gather | solution.py:181
  229.6 45.6 %scatter_custom_fusion.2 = s32[12288]{0:T(1024)S(1)} fusion(s32[12288]{0:T(1024)S(1)} %reshape.549, s32[12288]{0:T(1024)S(1)} %reshape.551, s32[]{:T(128)} %constant.101.clone.1), kind=kCustom, calls=%fused_computation.169 | custom fusion | bytes 49156
  276.5 1.6 fusion.47
  278.5 8.5 gather_fusion.4
  288.4 3.1 copy.220
  291.5 119.4 %gather_fusion.5 = bf16[12288,64]{1,0:T(8,128)(2,1)} fusion(bf16[1024,12,64]{2,0,1:T(8,128)(2,1)S(1)} %copy.220, s32[12288]{0:T(1024)S(1)} %reshape.603), kind=kCustom, calls=%fused_computation.3.clone | custom fusion | bytes 3244032 | tf_op jit(solution)/shard_map/jit(take_along_axis)/gather | solution.py:63
  410.9 6.6 reshape.614
  417.4 2.6 copy.209
  420.0 3.1 copy.211
  423.1 119.4 %gather_fusion.3 = bf16[12288,64]{1,0:T(8,128)(2,1)} fusion(bf16[1024,12,64]{2,0,1:T(8,128)(2,1)S(1)} %copy.211, s32[12288]{0:T(1024)S(1)} %reshape.603), kind=kCustom, calls=%fused_computation.clone | custom fusion | bytes 3244032 | tf_op jit(solution)/shard_map/jit(take_along_axis)/gather | solution.py:63
  542.4 6.6 reshape.606
  549.1 10.9 broadcast_select_fusion
  560.1 1.9 fusion.109
  565.2 8.5 gather_fusion.6
  574.6 1.8 fusion.110
  576.6 8.6 multiply_convert_fusion
  585.3 3.6 fusion.111
  590.9 2.4 fusion.102
  594.2 2.4 multiply_reduce_fusion.1
  599.0 8.5 gather_fusion.7
  608.8 1.8 convolution_bitcast_fusion
  610.6 3.1 copy.264
  613.7 119.4 %gather_fusion.10 = bf16[12288,64]{1,0:T(8,128)(2,1)} fusion(bf16[1024,12,64]{2,0,1:T(8,128)(2,1)S(1)} %bitcast.190, s32[12288]{0:T(1024)S(1)} %reshape.627), kind=kCustom, calls=%fused_computation.7.clone | custom fusion | bytes 3244032 | tf_op jit(solution)/shard_map/jit(take_along_axis)/gather | solution.py:63
  733.0 6.6 reshape.634
  739.6 5.8 copy.251
  745.4 4.0 fusion.1
  749.4 8.4 fusion.32
  758.5 1.8 multiply_bitcast_fusion
  760.3 3.1 copy.262
  763.4 119.4 %gather_fusion.9 = bf16[12288,64]{1,0:T(8,128)(2,1)} fusion(bf16[1024,12,64]{2,0,1:T(8,128)(2,1)S(1)} %bitcast.189, s32[12288]{0:T(1024)S(1)} %reshape.627), kind=kCustom, calls=%fused_computation.2.clone | custom fusion | bytes 3244032 | tf_op jit(solution)/shard_map/jit(take_along_axis)/gather | solution.py:63
  882.8 6.6 reshape.630
  889.4 5.3 copy.245
  894.6 2.8 select_convert_fusion.1
  901.7 3.1 fusion.36
  904.8 8.5 gather_fusion.8
  916.2 21.9 %reduce-scatter.25.cloned.1.call-done = bf16[128,768]{1,0:T(8,128)(2,1)} async-done(((bf16[1024,768]{1,0:T(8,128)(2,1)}), bf16[128,768]{1,0:T(8,128)(2,1)}) %reduce-scatter.25.cloned.1.call-update) | async-done | bytes 196624
  941.1 39.4 %reduce-scatter.27.cloned.1.call-done = bf16[128,768]{1,0:T(8,128)(2,1)} async-done(((bf16[1024,768]{1,0:T(8,128)(2,1)}), bf16[128,768]{1,0:T(8,128)(2,1)}) %reduce-scatter.27.cloned.1.call-update) | async-done | bytes 196624
  985.3 3.6 convolution_convert_fusion
  990.1 3.7 convolution_convert_fusion.1
  993.9 18.0 %reduce-scatter.29.cloned.1.call-done = bf16[192,768]{1,0:T(8,128)(2,1)} async-done(((bf16[768,768]{1,0:T(8,128)(2,1)}), bf16[192,768]{1,0:T(8,128)(2,1)}) %reduce-scatter.29.cloned.1.call-update) | async-done | bytes 294928
  1011.9 1.9 copy.270
  1013.8 28.4 %reduce-scatter.31.cloned.1.call-done = bf16[192,768]{1,0:T(8,128)(2,1)} async-done(((bf16[768,768]{1,0:T(8,128)(2,1)}), bf16[192,768]{1,0:T(8,128)(2,1)}) %reduce-scatter.31.cloned.1.call-update) | async-done | bytes 294928
  1042.1 1.9 copy.272
  1044.0 28.8 %reduce-scatter.33.cloned.1.call-done = bf16[192,768]{1,0:T(8,128)(2,1)} async-done(((bf16[768,768]{1,0:T(8,128)(2,1)}), bf16[192,768]{1,0:T(8,128)(2,1)}) %reduce-scatter.33.cloned.1.call-update) | async-done | bytes 294928
  1072.8 1.9 copy.274
  1074.7 28.4 %reduce-scatter.19.cloned.1.call-done = bf16[192,768]{1,0:T(8,128)(2,1)} async-done(((bf16[768,768]{1,0:T(8,128)(2,1)}), bf16[192,768]{1,0:T(8,128)(2,1)}) %reduce-scatter.19.cloned.1.call-update) | async-done | bytes 294928 | tf_op jit(solution)/shard_map/reduce_scatter | solution.py:288
  1103.0 86.2 %reduce-scatter.23.cloned.1.call-done = bf16[768,768]{1,0:T(8,128)(2,1)} async-done(((bf16[3072,768]{1,0:T(8,128)(2,1)}), bf16[768,768]{1,0:T(8,128)(2,1)}) %reduce-scatter.23.cloned.1.call-update) | async-done | bytes 1179664 | tf_op jit(solution)/shard_map/reduce_scatter | solution.py:312
  1189.2 88.0 %reduce-scatter.21.cloned.1.call-done = bf16[192,3072]{1,0:T(8,128)(2,1)} async-done(((bf16[768,3072]{1,0:T(8,128)(2,1)}), bf16[192,3072]{1,0:T(8,128)(2,1)}) %reduce-scatter.21.cloned.1.call-update) | async-done | bytes 1179664 | tf_op jit(solution)/shard_map/reduce_scatter | solution.py:306
  1282.8 18.8 %all-reduce.19 = (bf16[768]{0:T(1024)(128)(2,1)S(1)}, bf16[768]{0:T(1024)(128)(2,1)S(1)}, bf16[768]{0:T(1024)(128)(2,1)S(1)}, bf16[768]{0:T(1024)(128)(2,1)S(1)}...) all-reduce(bf16[768]{0:T(1024)(128)(2,1)} %copy-done.56, ...), channel_id=1, replica_groups=mesh['ctx'=8,'fsdp'=4] {'fsdp'}, use_global_device_ids=true, to_apply=%add.7 | all-reduce | flops 9984 | bytes 39936
  1302.3 12.0 all-reduce.17
  1320.1 2.6 fusion.49
  1323.5 38.1 %all-reduce.23.cloned.1.call-done = (bf16[192,768]{0,1:T(8,128)(2,1)}, bf16[192,768]{0,1:T(8,128)(2,1)}, bf16[192,768]{0,1:T(8,128)(2,1)}, bf16[192,768]{1,0:T(8...) async-done(((bf16[192,768]{0,1:T(8,128)(2,1)}, bf16[192,768]{0,1:T(8,128)(2,1)}, bf16[192,768]{0,1:T(8,128)(2,1)}, bf16[192,768]{1,0:T(8,128)(2,1)}, ...) | async-done | bytes 3538960 | tf_op jit(solution)/shard_map/psum | solution.py:326
  1361.6 3.0 convert_element_type.296
  (362 shorter events, 64.1 us)
Async XLA Ops:
  7.2 140.1 %copy-start = (s32[1,1024]{1,0:T(1,128)S(1)}, s32[1,1024]{1,0:T(1,128)}, u32[]{:S(2)}) copy-start(s32[1,1024]{1,0:T(1,128)} %param.27) | copy-start | bytes 12292
  7.2 15.7 %copy-start.23 = (bf16[192,768]{1,0:T(8,128)(2,1)S(1)}, bf16[192,768]{1,0:T(8,128)(2,1)}, u32[]{:S(2)}) copy-start(bf16[192,768]{1,0:T(8,128)(2,1)} %param.30) | copy-start | bytes 884740
  7.2 83.5 %all-gather.9.cloned.1.call-start = ((), (), s32[]{:S(2)}) async-start(), calls=%async_computation.8 | async-start | bytes 1474560 | tf_op jit(solution)/shard_map/all_gather | solution.py:170
  7.9 268.5 %all-gather.13.cloned.1.call-start = ((), (), s32[]{:S(2)}) async-start(), calls=%async_computation.10 | async-start | bytes 1474560 | tf_op jit(solution)/shard_map/all_gather | solution.py:168
  8.7 279.7 %all-gather.15.cloned.1.call-start = ((), (), s32[]{:S(2)}) async-start(), calls=%async_computation.11 | async-start | bytes 1769472 | tf_op jit(solution)/shard_map/all_gather | solution.py:201
  8.7 11.7 collective-permute-start
  21.4 46.5 %collective-permute-start.1 = (bf16[384,768]{1,0:T(8,128)(2,1)S(1)}, bf16[384,768]{1,0:T(8,128)(2,1)S(1)}, u32[]{:S(2)}, u32[]{:S(2)}) collective-permute-start(bf16[384,768]{1,0:T(8,128)(2,1)S(1)} %pad_maximum_fusion), channel_id=1, source_target_pairs={{0,2},{1,3},{2,0},{3,1},{4,6},{5,7},{6,4},{7,5},{8,10},{9,11},{10,... | collective-permute-start | bytes 1769480 | tf_op jit(solution)/shard_map/ppermute | solution.py:18
  22.9 46.6 %copy-start.8 = (bf16[1,128,768]{2,1,0:T(8,128)(2,1)S(1)}, bf16[1,128,768]{2,1,0:T(8,128)(2,1)}, u32[]{:S(2)}) copy-start(bf16[1,128,768]{2,1,0:T(8,128)(2,1)} %param.25) | copy-start | bytes 589828
  68.0 4.1 copy-start.68
  68.0 4.3 copy-start.69
  68.0 4.6 copy-start.70
  68.0 4.8 copy-start.71
  68.1 5.0 copy-start.72
  68.1 5.2 copy-start.73
  68.1 5.4 copy-start.74
  70.8 346.7 %all-gather.11.cloned.1.call-start = ((), (), s32[]{:S(2)}) async-start(), calls=%async_computation.9 | async-start | bytes 1769472 | tf_op jit(solution)/shard_map/all_gather | solution.py:202
  93.1 5.8 copy-start.61
  93.1 5.8 copy-start.67
  93.1 481.5 %all-gather.17.cloned.1.call-start = ((), (), s32[]{:S(2)}) async-start(), calls=%async_computation.12 | async-start | bytes 1474560 | tf_op jit(solution)/shard_map/all_gather | solution.py:171
  93.7 5.6 copy-start.62
  93.7 5.6 copy-start.66
  93.7 482.9 %all-gather.19.cloned.1.call-start = ((), (), s32[]{:S(2)}) async-start(), calls=%async_computation.13 | async-start | bytes 5898240 | tf_op jit(solution)/shard_map/all_gather | solution.py:179
  94.3 491.0 %all-gather.21.cloned.1.call-start = ((), (), s32[]{:S(2)}) async-start(), calls=%async_computation.14 | async-start | bytes 5898240 | tf_op jit(solution)/shard_map/all_gather | solution.py:180
  95.0 843.1 %reduce-scatter.25.cloned.1.call-start = ((), (), s32[]{:S(2)}) async-start(), calls=%async_computation.18 | async-start | bytes 1769472
  158.4 55.9 %copy-start.64 = (bf16[768]{0:T(1024)(128)(2,1)S(1)}, bf16[768]{0:T(1024)(128)(2,1)}, u32[]{:S(2)}) copy-start(bf16[768]{0:T(1024)(128)(2,1)} %param.39) | copy-start | bytes 4612
  542.4 6.6 copy-start.41
  549.1 11.0 copy-start.31
  549.1 11.0 copy-start.37
  560.0 5.1 copy-start.3
  576.4 20.3 %copy-start.4 = (f32[128,768]{1,0:T(8,128)}, f32[128,768]{1,0:T(8,128)S(1)}, u32[]{:S(2)}) copy-start(f32[128,768]{1,0:T(8,128)S(1)} %get-tuple-element.175) | copy-start | bytes 1179652
  576.6 20.1 %copy-start.50 = (f32[128]{0:T(128)}, f32[128]{0:T(128)S(1)}, u32[]{:S(2)}) copy-start(f32[128]{0:T(128)S(1)} %fusion.97) | copy-start | bytes 1540
  576.6 8.6 copy-start.49
  585.2 3.7 copy-start.11
  585.3 5.6 slice-start.2
  585.3 3.9 copy-start.29
  585.3 5.6 slice-start.3
  585.3 5.6 copy-start.77
  589.0 4.4 copy-start.57
  589.2 4.2 copy-start.59
  590.2 4.0 slice-start
  590.9 3.3 slice-start.1
  739.6 5.8 copy-start.32
  745.4 4.0 copy-start.10
  745.4 4.0 copy-start.47
  749.4 9.1 copy-start.17
  889.4 5.3 copy-start.48
  899.0 81.5 %reduce-scatter.27.cloned.1.call-start = ((), (), s32[]{:S(2)}) async-start(), calls=%async_computation.19 | async-start | bytes 1769472
  900.7 111.2 %reduce-scatter.29.cloned.1.call-start = ((), (), s32[]{:S(2)}) async-start(), calls=%async_computation.20 | async-start | bytes 1474560
  916.2 125.9 %reduce-scatter.31.cloned.1.call-start = ((), (), s32[]{:S(2)}) async-start(), calls=%async_computation.21 | async-start | bytes 1474560
  941.0 131.7 %reduce-scatter.33.cloned.1.call-start = ((), (), s32[]{:S(2)}) async-start(), calls=%async_computation.22 | async-start | bytes 1474560
  983.5 119.6 %reduce-scatter.19.cloned.1.call-start = ((), (), s32[]{:S(2)}) async-start(), calls=%async_computation.15 | async-start | bytes 1474560 | tf_op jit(solution)/shard_map/reduce_scatter | solution.py:288
  985.1 204.2 %reduce-scatter.23.cloned.1.call-start = ((), (), s32[]{:S(2)}) async-start(), calls=%async_computation.17 | async-start | bytes 5898240 | tf_op jit(solution)/shard_map/reduce_scatter | solution.py:312
  988.9 288.3 %reduce-scatter.21.cloned.1.call-start = ((), (), s32[]{:S(2)}) async-start(), calls=%async_computation.16 | async-start | bytes 5898240 | tf_op jit(solution)/shard_map/reduce_scatter | solution.py:306
  993.8 367.8 %all-reduce.23.cloned.1.call-start = ((), (), s32[]{:S(2)}) async-start(), calls=%async_computation.23 | async-start | bytes 7667712 | tf_op jit(solution)/shard_map/psum | solution.py:326
  1277.2 4.4 copy-start.14
  1277.2 4.4 copy-start.19
  1278.1 4.6 copy-start.24
  1278.1 4.7 copy-start.53
  1278.1 4.7 copy-start.54
  1278.1 4.7 copy-start.55
  1278.1 41.4 %copy-start.13 = (bf16[768,768]{1,0:T(8,128)(2,1)S(1)}, bf16[768,768]{1,0:T(8,128)(2,1)}, u32[]{:S(2)}) copy-start(bf16[768,768]{1,0:T(8,128)(2,1)} %all-gather.9.cloned.1.call-done) | copy-start | bytes 3538948
  1282.7 37.3 %copy-start.38 = (bf16[128,768]{1,0:T(8,128)(2,1)S(1)}, bf16[128,768]{1,0:T(8,128)(2,1)}, u32[]{:S(2)}) copy-start(bf16[128,768]{1,0:T(8,128)(2,1)} %reduce-scatter.25.cloned.1.call-done) | copy-start | bytes 589828
  1361.6 3.0 copy-start.36
  1366.2 3.8 copy-start.1
  (36 other events, 61.8 us)
Sparse Core Ops, SparseCore 0:
  9.6 55.0 all-gather.8
  66.3 29.0 all-gather.12
  97.9 25.0 all-gather.14
  125.3 25.6 all-gather.10
  152.4 30.4 all-gather.16
  184.3 88.6 all-gather.18
  274.6 87.8 all-gather.20
  899.2 38.9 reduce-scatter.24
  942.0 38.4 reduce-scatter.26
  982.7 29.1 reduce-scatter.28
  1014.2 27.8 reduce-scatter.30
  1044.9 27.8 reduce-scatter.32
  1075.1 27.8 reduce-scatter.18
  1105.2 83.9 reduce-scatter.22
  1191.4 85.7 reduce-scatter.20
  1282.3 79.2 all-reduce.22
